TPU v7x, 512 devices: a whole 4x8x8 slice. The times are simulated.
512 devices in a mesh: ctx: 32 (over z, y_lo), tp: 16 (over x, y_hi, core).
Axes of the slice: x: 4, y: 8 (y_hi: 2, y_lo: 4; y = y_hi * 4 + y_lo), z: 8, core: 2. Of those that a mesh axis runs over, the one named last changes fastest.
Arguments:
- queries: bfloat16 [4096, 6144], P('ctx', 'tp'), may hold values from -6 to 6
- keys: bfloat16 [4096, 6144], P('ctx', 'tp'), may hold values from -6 to 6
- values: bfloat16 [4096, 6144], P('ctx', 'tp'), may hold values from -6 to 6
- norm_gain: float32 [6144], P('tp'), may hold values from 0.1 to 1.9
- out_weight: bfloat16 [6144, 6144], P('tp', 'ctx'), may hold values from -0.15625 to 0.15625
Outputs:
- projected: bfloat16 [4096, 6144], P('ctx', 'tp')
All inputs are finite; a program needn't handle non-finite values.
Results may differ from a plain program's by a relative error of at most 0.017.
Values may be sent and summed in bfloat16 or wider, within the bound.
A program may use at most 64 MiB of HBM per device.

v0:
```python
import jax
import jax.numpy as jnp
from jax import lax
from jax.sharding import PartitionSpec as P

HS = 128


def prefix(x, axis, combine, identity):
    count, index = (lax.axis_size(axis), lax.axis_index(axis))
    everything = lax.all_gather(x.astype(jnp.bfloat16), axis)
    start = jnp.broadcast_to(jnp.asarray(identity, x.dtype), x.shape)

    def step(k, before):
        reached = k < index
        new = combine(before, everything[k].astype(x.dtype))
        return jnp.where(reached, new, before)

    return lax.fori_loop(0, count, step, start)


def add_states(earlier, later):
    return earlier + later


def carried_state(local_state):
    return prefix(local_state, "ctx", add_states, jnp.zeros_like(local_state))


def body(queries, keys, values, norm_gain, out_weight):
    tokens_here = queries.shape[0]
    features = queries.shape[1]
    heads_here = features // HS
    query_heads = queries.reshape(tokens_here, heads_here, HS)
    key_heads = keys.reshape(tokens_here, heads_here, HS)
    value_heads = values.reshape(tokens_here, heads_here, HS)
    local_state = jnp.einsum(
        "shd,she->hde", key_heads, value_heads, preferred_element_type=jnp.float32
    )
    scores = jnp.einsum("thd,shd->hts", query_heads, key_heads, preferred_element_type=jnp.float32)
    rows_index = lax.broadcasted_iota(jnp.int32, (tokens_here, tokens_here), 0)
    cols_index = lax.broadcasted_iota(jnp.int32, (tokens_here, tokens_here), 1)
    causal = rows_index >= cols_index
    scores = jnp.where(causal[None], scores, jnp.float32(0.0)).astype(jnp.bfloat16)
    within = jnp.einsum("hts,shd->thd", scores, value_heads, preferred_element_type=jnp.float32)
    prefix_state = carried_state(local_state)
    carried = jnp.einsum(
        "thd,hde->the",
        query_heads.astype(jnp.float32),
        prefix_state,
        precision=lax.Precision.HIGHEST,
    )
    mixed_sum = within + carried
    inverse_rms = lax.rsqrt(jnp.mean(mixed_sum * mixed_sum, axis=-1, keepdims=True) + 1e-06)
    attended = (mixed_sum * inverse_rms * norm_gain.reshape(heads_here, HS)).astype(jnp.bfloat16)
    attended = attended.reshape(tokens_here, features)
    partials = jnp.dot(
        attended,
        lax.all_gather(out_weight, "ctx", axis=1, tiled=True),
        preferred_element_type=jnp.float32,
    )
    return lax.psum_scatter(partials.astype(jnp.bfloat16), "tp", scatter_dimension=1, tiled=True)


def solution(mesh):
    return jax.shard_map(
        body,
        mesh=mesh,
        in_specs=(P("ctx", "tp"), P("ctx", "tp"), P("ctx", "tp"), P("tp"), P("tp", "ctx")),
        out_specs=P("ctx", "tp"),
        check_vma=False,
    )
```

profile of v0, /device:TPU:2, one launch (start us, length us, event | category | flops | bytes accessed | tf_op | source)
XLA Modules:
  0.0 449.8 jit_solution(4256987266796342964)
XLA Ops:
  6.5 1.0 copy.18
  7.6 1.0 copy.21
  8.6 0.8 convolution_convert_fusion.1
  9.4 0.0 all-gather.4.cloned.1.call-start
  9.5 0.7 all-gather.4.cloned.1.call-update
  10.3 1.0 copy.17
  11.3 0.4 convolution_bitcast_fusion.1
  11.7 164.5 %all-gather.6.cloned.1.call-done = bf16[96,128,128]{2,1,0:T(8,128)(2,1)} async-done(((bf16[3,128,128]{2,1,0:T(8,128)(2,1)}), bf16[96,128,128]{2,1,0:T(8,128)(2,1)}) %all-gather.6.cloned.1.call-update) | async-done | bytes 3145744 | tf_op jit(solution)/shard_map/all_gather | solution.py:11
  176.2 32.3 %while.14 = (s32[]{:T(128)}, f32[3,128,128]{2,1,0:T(8,128)S(1)}, s32[]{:T(128)}, bf16[32,3,128,128]{3,2,1,0:T(8,128)(2,1)}, s32[]{:T(128)}, /*index=5*/s32[]{:T(128)}) while((s32[]{:T(128)}, f32[3,128,128]{2,1,0:T(8,128)S(1)}, s32[]{:T(128)}, bf16[32,3,128,128]{3,2,1,0:T(8,128)(2,1)}, s32[]{:T(128)}, /*index=5*/s32[]{:T(128)}) %tuple.42), condition=%wide.region_1.2_spmd.clone, body=%wide.region_0.1_spmd.clone.sunk | while | flops 196612 | bytes 491613 | solution.py:19
  176.2 1.0 add_select_fusion.2
  177.2 1.0 add_select_fusion.2
  178.2 1.0 add_select_fusion.2
  179.2 1.0 add_select_fusion.2
  180.2 1.0 add_select_fusion.2
  181.2 1.0 add_select_fusion.2
  182.2 1.0 add_select_fusion.2
  183.2 1.0 add_select_fusion.2
  184.3 1.0 add_select_fusion.2
  185.3 1.0 add_select_fusion.2
  186.3 1.0 add_select_fusion.2
  187.3 1.0 add_select_fusion.2
  188.3 1.0 add_select_fusion.2
  189.3 1.0 add_select_fusion.2
  190.3 1.0 add_select_fusion.2
  191.3 1.0 add_select_fusion.2
  192.3 1.0 add_select_fusion.2
  193.3 1.0 add_select_fusion.2
  194.3 1.0 add_select_fusion.2
  195.4 1.0 add_select_fusion.2
  196.4 1.0 add_select_fusion.2
  197.4 1.0 add_select_fusion.2
  198.4 1.0 add_select_fusion.2
  199.4 1.0 add_select_fusion.2
  200.4 1.0 add_select_fusion.2
  201.4 1.0 add_select_fusion.2
  202.4 1.0 add_select_fusion.2
  203.4 1.0 add_select_fusion.2
  204.4 1.0 add_select_fusion.2
  205.4 1.0 add_select_fusion.2
  206.5 1.0 add_select_fusion.2
  207.5 1.0 add_select_fusion.2
  208.5 0.4 multiply_reduce_fusion
  208.9 0.1 multiply_convert_fusion
  209.0 137.4 %all-gather.4.cloned.1.call-done = bf16[384,6144]{0,1:T(8,128)(2,1)} async-done(((bf16[384,192]{0,1:T(8,128)(2,1)}), bf16[384,6144]{0,1:T(8,128)(2,1)}) %all-gather.4.cloned.1.call-update) | async-done | bytes 4718608 | tf_op jit(solution)/shard_map/all_gather | solution.py:59
  346.4 4.0 convolution_convert_fusion
  350.4 1.6 copy.30
  352.0 89.6 %reduce-scatter.4.cloned.1.call-done = bf16[384,128]{1,0:T(8,128)(2,1)} async-done(((bf16[6144,128]{1,0:T(8,128)(2,1)}), bf16[384,128]{1,0:T(8,128)(2,1)}) %reduce-scatter.4.cloned.1.call-update) | async-done | bytes 98320
  441.6 1.6 copy.31
  (9 shorter events, 0.1 us)
Async XLA Ops:
  6.5 202.3 %copy-start = (f32[384]{0:T(512)S(1)}, f32[384]{0:T(512)}, u32[]{:S(2)}) copy-start(f32[384]{0:T(512)} %param.10) | copy-start | bytes 4612
  6.5 169.7 %all-gather.6.cloned.1.call-start = ((), (), s32[]{:S(2)}) async-start(), calls=%async_computation.2 | async-start | bytes 3244032 | tf_op jit(solution)/shard_map/all_gather | solution.py:11
  9.4 337.0 %all-gather.4.cloned.1.call-start = ((), (), s32[]{:S(2)}) async-start(), calls=%async_computation.1 | async-start | bytes 4866048 | tf_op jit(solution)/shard_map/all_gather | solution.py:59
  10.2 431.4 %reduce-scatter.4.cloned.1.call-start = ((), (), s32[]{:S(2)}) async-start(), calls=%async_computation.3 | async-start | bytes 1671168
Sparse Core Ops, SparseCore 0:
  9.6 166.5 all-gather.5
  178.3 168.1 all-gather.3
  352.1 89.4 reduce-scatter.3
where the time goes:
time: 451 us; the launch traced here: 450 us
  waiting for transfers between devices  392 us (87%)
  other arithmetic  31.7 us (7%)
  between operations  13.2 us (3%)
  local copies, waits for them, and re-layouts  6.25 us (1%)
  matrix products  5.57 us (1%)
    all_gather x1, waiting for transfers between devices, prefix(): everything = lax.all_gather(x.astype(jnp.bfloat16), axis)  165 us
    all_gather x1, waiting for transfers between devices, body(): lax.all_gather(out_weight, 'ctx', axis=1, tiled=True)  137 us
    unnamed x4, waiting for transfers between devices  90.3 us
    select_n x32, other arithmetic, step(): return jnp.where(reached, new, before)  31.6 us
  transfers between devices with their start and end apart: 3, of which 3 were waited for; matrix products, arithmetic and copies ran while one was open for 7% of the time, Pallas kernels for 0%

commit v1 on v0

--- a/solution.py
+++ b/solution.py
@@ -2,8 +2,16 @@
 import jax.numpy as jnp
 from jax import lax
 from jax.sharding import PartitionSpec as P
+from jax.lax import all_to_all, axis_size
 
 HS = 128
+
+
+def pair_task(tile_in, axis_key):
+    block_out = tuple((tile_in for _ in range(axis_size(axis_key))))
+    y = jnp.stack(block_out)
+    f_now = all_to_all(y, axis_key, 0, 0)
+    return jnp.concatenate(f_now, axis=1)
 
 
 def prefix(x, axis, combine, identity):
@@ -54,11 +62,7 @@
     inverse_rms = lax.rsqrt(jnp.mean(mixed_sum * mixed_sum, axis=-1, keepdims=True) + 1e-06)
     attended = (mixed_sum * inverse_rms * norm_gain.reshape(heads_here, HS)).astype(jnp.bfloat16)
     attended = attended.reshape(tokens_here, features)
-    partials = jnp.dot(
-        attended,
-        lax.all_gather(out_weight, "ctx", axis=1, tiled=True),
-        preferred_element_type=jnp.float32,
-    )
+    partials = jnp.dot(attended, pair_task(out_weight, "ctx"), preferred_element_type=jnp.float32)
     return lax.psum_scatter(partials.astype(jnp.bfloat16), "tp", scatter_dimension=1, tiled=True)
 
 

time: 451 us -> 392 us (0.87)
  waiting for transfers between devices: 392 us -> 316 us
  starting transfers between devices: 0.08 us -> 14 us
    all_gather x1 -> x0, waiting for transfers between devices: 137 us -> none  [body(): lax.all_gather(out_weight, 'ctx', axis=1, tiled=True)]
    all_gather x1, waiting for transfers between devices: 165 us -> 207 us  [prefix(): everything = lax.all_gather(x.astype(jnp.bfloat16), axis)]
    unnamed x4 -> x3, waiting for transfers between devices: 90.3 us -> 109 us
    all_to_all x0 -> x1, starting transfers between devices: none -> 14 us  [pair_task(): f_now = all_to_all(y, axis_key, 0, 0)]
  transfers between devices with their start and end apart: 3 -> 3, of which waited for: 3 -> 2; matrix products, arithmetic and copies ran while one was open for 7% -> 9% of each run, Pallas kernels for 0% -> 0%
where the time goes in v1:
time: 392 us; the launch traced here: 391 us
  waiting for transfers between devices  316 us (81%)
  other arithmetic  31.7 us (8%)
  starting transfers between devices  14 us (4%)
  between operations  13.5 us (3%)
  local copies, waits for them, and re-layouts  9.15 us (2%)
  matrix products  5.53 us (1%)
    all_gather x1, waiting for transfers between devices, prefix(): everything = lax.all_gather(x.astype(jnp.bfloat16), axis)  207 us
    unnamed x3, waiting for transfers between devices  109 us
    select_n x32, other arithmetic, step(): return jnp.where(reached, new, before)  31.6 us
    all_to_all x1, starting transfers between devices, pair_task(): f_now = all_to_all(y, axis_key, 0, 0)  14 us
  transfers between devices with their start and end apart: 3, of which 2 were waited for; matrix products, arithmetic and copies ran while one was open for 9% of the time, Pallas kernels for 0%

profile of v1, /device:TPU:2, one launch (start us, length us, event | category | flops | bytes accessed | tf_op | source)
XLA Modules:
  0.0 390.9 jit_solution(8363685247034319548)
XLA Ops:
  6.5 1.0 copy.19
  7.5 1.0 copy.22
  8.6 0.8 convolution_convert_fusion.1
  9.4 3.8 stack.2
  13.2 14.0 %all-to-all-start = ((bf16[32,384,192]{1,2,0:T(8,128)(2,1)}), bf16[32,384,192]{1,2,0:T(8,128)(2,1)}, u32[]{:S(2)}, u32[]{:S(2)}) async-start(bf16[32,384,192]{1,2,0:T(8,128)(2,1)} %stack.2), calls=%async_computation | async-start | bytes 9437184 | tf_op jit(solution)/shard_map/all_to_all | solution.py:13
  27.2 0.0 reduce-scatter.4.cloned.1.call-start
  27.3 0.1 copy.18
  27.5 0.4 convolution_bitcast_fusion.1
  27.9 206.9 %all-gather.3.cloned.1.call-done = bf16[96,128,128]{2,1,0:T(8,128)(2,1)} async-done(((bf16[3,128,128]{2,1,0:T(8,128)(2,1)}), bf16[96,128,128]{2,1,0:T(8,128)(2,1)}) %all-gather.3.cloned.1.call-update) | async-done | bytes 3145744 | tf_op jit(solution)/shard_map/all_gather | solution.py:19
  234.8 32.3 %while.14 = (s32[]{:T(128)}, f32[3,128,128]{2,1,0:T(8,128)S(1)}, s32[]{:T(128)}, bf16[32,3,128,128]{3,2,1,0:T(8,128)(2,1)}, s32[]{:T(128)}, /*index=5*/s32[]{:T(128)}) while((s32[]{:T(128)}, f32[3,128,128]{2,1,0:T(8,128)S(1)}, s32[]{:T(128)}, bf16[32,3,128,128]{3,2,1,0:T(8,128)(2,1)}, s32[]{:T(128)}, /*index=5*/s32[]{:T(128)}) %tuple.40), condition=%wide.region_1.2_spmd.clone, body=%wide.region_0.1_spmd.clone.sunk | while | flops 196612 | bytes 491621 | solution.py:27
  234.8 1.0 add_select_fusion.2
  235.8 1.0 add_select_fusion.2
  236.8 1.0 add_select_fusion.2
  237.8 1.0 add_select_fusion.2
  238.8 1.0 add_select_fusion.2
  239.8 1.0 add_select_fusion.2
  240.8 1.0 add_select_fusion.2
  241.9 1.0 add_select_fusion.2
  242.9 1.0 add_select_fusion.2
  243.9 1.0 add_select_fusion.2
  244.9 1.0 add_select_fusion.2
  245.9 1.0 add_select_fusion.2
  246.9 1.0 add_select_fusion.2
  247.9 1.0 add_select_fusion.2
  248.9 1.0 add_select_fusion.2
  249.9 1.0 add_select_fusion.2
  250.9 1.0 add_select_fusion.2
  251.9 1.0 add_select_fusion.2
  253.0 1.0 add_select_fusion.2
  254.0 1.0 add_select_fusion.2
  255.0 1.0 add_select_fusion.2
  256.0 1.0 add_select_fusion.2
  257.0 1.0 add_select_fusion.2
  258.0 1.0 add_select_fusion.2
  259.0 1.0 add_select_fusion.2
  260.0 1.0 add_select_fusion.2
  261.0 1.0 add_select_fusion.2
  262.0 1.0 add_select_fusion.2
  263.0 1.0 add_select_fusion.2
  264.1 1.0 add_select_fusion.2
  265.1 1.0 add_select_fusion.2
  266.1 1.0 add_select_fusion.2
  267.1 0.4 multiply_reduce_fusion
  267.5 0.1 multiply_convert_fusion
  267.6 3.9 %convolution_convert_fusion = bf16[128,6144]{1,0:T(8,128)(2,1)S(1)} fusion(bf16[128,384]{0,1:T(8,128)(2,1)S(1)} %bitcast.38, bf16[384,6144]{0,1:T(8,128)(2,1)} %bitcast.9), kind=kOutput, calls=%fused_computation.1 | convolution fusion | flops 604766208 | bytes 6389760 | tf_op jit(solution)/shard_map/dot_general | solution.py:65
  271.5 1.6 copy.31
  273.1 109.3 %reduce-scatter.4.cloned.1.call-done = bf16[384,128]{1,0:T(8,128)(2,1)} async-done(((bf16[6144,128]{1,0:T(8,128)(2,1)}), bf16[384,128]{1,0:T(8,128)(2,1)}) %reduce-scatter.4.cloned.1.call-update) | async-done | bytes 98320
  382.5 1.6 copy.32
  (11 shorter events, 0.1 us)
Async XLA Ops:
  6.5 228.3 %all-gather.3.cloned.1.call-start = ((), (), s32[]{:S(2)}) async-start(), calls=%async_computation.2 | async-start | bytes 3244032 | tf_op jit(solution)/shard_map/all_gather | solution.py:19
  13.2 14.1 %copy-start = (bf16[128,384]{1,0:T(8,128)(2,1)S(1)}, bf16[128,384]{1,0:T(8,128)(2,1)}, u32[]{:S(2)}) copy-start(bf16[128,384]{1,0:T(8,128)(2,1)} %param.7) | copy-start | bytes 294916
  13.2 254.4 %all-to-all-start = ((bf16[32,384,192]{1,2,0:T(8,128)(2,1)}), bf16[32,384,192]{1,2,0:T(8,128)(2,1)}, u32[]{:S(2)}, u32[]{:S(2)}) async-start(bf16[32,384,192]{1,2,0:T(8,128)(2,1)} %stack.2), calls=%async_computation | async-start | bytes 9437184 | tf_op jit(solution)/shard_map/all_to_all | solution.py:13
  27.2 240.2 %copy-start.1 = (f32[384]{0:T(512)S(1)}, f32[384]{0:T(512)}, u32[]{:S(2)}) copy-start(f32[384]{0:T(512)} %param.10) | copy-start | bytes 4612
  27.2 355.2 %reduce-scatter.4.cloned.1.call-start = ((), (), s32[]{:S(2)}) async-start(), calls=%async_computation.3 | async-start | bytes 1671168
Sparse Core Ops, SparseCore 0:
  9.6 225.2 all-gather.2
  273.2 109.1 reduce-scatter.3
